TPU v7x, 128 devices: a whole 4x4x4 slice. The times are simulated.
128 devices in a mesh: row: 8 (over x_lo, z), col: 16 (over x_hi, y, core).
Axes of the slice: x: 4 (x_hi: 2, x_lo: 2; x = x_hi * 2 + x_lo), y: 4, z: 4, core: 2. Of those that a mesh axis runs over, the one named last changes fastest.
Arguments:
- tokens: bfloat16 [2048, 4096], P('row', 'col'), may hold values from -6 to 6
- norm_gain: float32 [4096], replicated, may hold values from 0.1 to 1.9
- expert_ids: int32 [2048, 2], P('row'), may hold values from 0 to 7, all different within a row; in each aligned block of 256 rows (0 to 255, 256 to 511, ...) at most 128 rows name the same one
- gate_weights: float32 [2048, 2], P('row'), may hold values from 0.1 to 1
- w_gate: bfloat16 [8, 4096, 14336], P('row', None, 'col'), may hold values from -0.09375 to 0.09375
- w_up: bfloat16 [8, 4096, 14336], P('row', None, 'col'), may hold values from -0.09375 to 0.09375
- w_down: bfloat16 [8, 14336, 4096], P('row', 'col'), may hold values from -0.046875 to 0.046875
Outputs:
- layer_output: bfloat16 [2048, 4096], P('row', 'col')
Inputs may be any that keep to these rules, and one draw needn't show every extreme that they name: `expert_ids`: the 2 experts of a token differ. In each aligned block of 256 tokens no expert is chosen by more than 128 tokens, a bound that some block reaches.
All inputs are finite; a program needn't handle non-finite values.
Results may differ from a plain program's by a relative error of at most 0.0043.
Values may be sent and summed in bfloat16 or wider, within the bound.
A program may use at most 128 MiB of HBM per device.

v0:
```python
import jax
import jax.numpy as jnp
from jax import lax
from jax.sharding import PartitionSpec as P

EXPERTS = 8
CAP = 128


def normalize(rows, norm_gain):
    values = rows.astype(jnp.float32)
    inverse_norm = lax.rsqrt(jnp.mean(values * values, axis=-1, keepdims=True) + 1e-05)
    return (values * inverse_norm * norm_gain).astype(jnp.bfloat16)


def route_tables(expert_ids, expert_count, capacity):
    token_count = expert_ids.shape[0]
    flat_ids = expert_ids.reshape(-1)
    expert_range = jnp.arange(expert_count, dtype=jnp.int32)
    expert_hits = (flat_ids[:, None] == expert_range[None, :]).astype(jnp.int32)
    earlier = jnp.cumsum(expert_hits, axis=0) - expert_hits
    ranks = jnp.sum(earlier * expert_hits, axis=1)
    slot_index = (flat_ids * capacity + ranks).reshape(token_count, -1)
    slot_ids = jnp.arange(expert_count * capacity, dtype=jnp.int32)
    matches = (slot_index[:, :, None] == slot_ids[None, None, :]).astype(jnp.float32)
    picker = jnp.sum(matches, axis=1)
    return (picker.astype(jnp.bfloat16), slot_index)


def combine_rows(slot_rows, slot_index, gate_weights):
    picked = slot_rows[slot_index]
    return jnp.sum(picked * gate_weights[:, :, None], axis=1)


def run_experts(normed, gate_block, up_block, down_block):
    local_count = gate_block.shape[0]
    sources = normed.shape[0] // local_count
    grouped = normed.reshape(sources, local_count, normed.shape[1], normed.shape[2])
    gate_part = jnp.einsum(
        "slcd,ldf->slcf", grouped, gate_block, preferred_element_type=jnp.float32
    )
    up_part = jnp.einsum("slcd,ldf->slcf", grouped, up_block, preferred_element_type=jnp.float32)
    hidden = (jax.nn.silu(gate_part) * up_part).astype(jnp.bfloat16)
    outputs = jnp.einsum("slcf,lfd->slcd", hidden, down_block, preferred_element_type=jnp.float32)
    return outputs.reshape(normed.shape[0], normed.shape[1], down_block.shape[2])


def body(tokens, norm_gain, expert_ids, gate_weights, w_gate, w_up, w_down):
    picker, slot_index = route_tables(expert_ids, EXPERTS, CAP)
    packed = jnp.einsum("ts,td->sd", picker, tokens, preferred_element_type=jnp.float32).astype(
        jnp.bfloat16
    )
    packed = packed.reshape(EXPERTS, CAP, tokens.shape[1])
    arrived = lax.all_to_all(packed, "row", split_axis=0, concat_axis=0, tiled=True)
    widened = lax.all_gather(arrived, "col", axis=2, tiled=True)
    normed = normalize(widened, norm_gain)
    outputs = run_experts(normed, w_gate, w_up, w_down)
    shares = lax.psum_scatter(outputs, "col", scatter_dimension=2, tiled=True)
    returned = lax.all_to_all(shares, "row", split_axis=0, concat_axis=0, tiled=True)
    mixed = combine_rows(returned.reshape(-1, shares.shape[2]), slot_index, gate_weights)
    return (tokens.astype(jnp.float32) + mixed).astype(jnp.bfloat16)


def solution(mesh):
    placed = (
        P("row", "col"),
        P(),
        P("row", None),
        P("row", None),
        P("row", None, "col"),
        P("row", None, "col"),
        P("row", "col", None),
    )
    return jax.shard_map(
        body, mesh=mesh, in_specs=placed, out_specs=P("row", "col"), check_vma=False
    )
```

profile of v0, /device:TPU:0, one launch (start us, length us, event | category | flops | bytes accessed | tf_op | source)
XLA Modules:
  0.0 323.9 jit_solution(4479239125791643411)
XLA Ops:
  6.5 0.0 copy-start.3
  6.5 0.0 all-gather.2.cloned.1.call-start
  6.5 0.8 copy.21
  7.4 0.1 eq.42
  7.5 0.1 eq.38
  7.7 1.1 reduce-window.6
  8.8 0.2 slice_reduce_fusion
  9.1 0.1 fusion.30
  9.2 0.1 reduce_sum.39
  9.3 0.1 copy.23
  9.4 0.7 compare_select_fusion
  10.1 0.3 convert_reduce_fusion
  10.4 1.3 convolution_convert_fusion
  11.6 16.3 %all_to_all.10 = bf16[8,128,256]{2,1,0:T(8,128)(2,1)} all-to-all(bf16[8,128,256]{2,1,0:T(8,128)(2,1)S(1)} %bitcast.67), channel_id=1, replica_groups=mesh['row'=8,'col'=16] {'row'}, dimensions={0} | all-to-all | bytes 1048576 | tf_op jit(solution)/shard_map/all_to_all | solution.py:54
  27.9 0.0 all-gather.2.cloned.1.call-update
  27.9 0.0 reduce-scatter.2.cloned.1.call-start
  28.0 76.0 %all-gather.2.cloned.1.call-done = bf16[8,128,4096]{2,1,0:T(8,128)(2,1)} async-done(((bf16[8,128,256]{2,1,0:T(8,128)(2,1)}), bf16[8,128,4096]{2,1,0:T(8,128)(2,1)}) %all-gather.2.cloned.1.call-update) | async-done | bytes 8388624 | tf_op jit(solution)/shard_map/all_gather | solution.py:55
  104.0 0.0 copy-start
  104.0 5.2 %fusion = f32[8,128]{1,0:T(8,128)S(1)} fusion(bf16[8,128,4096]{2,1,0:T(8,128)(2,1)} %all-gather.2.cloned.1.call-done), kind=kLoop, calls=%fused_computation.3 | loop fusion | flops 12581888 | bytes 8392704 | tf_op jit(solution)/shard_map/reduce_sum | solution.py:12
  109.3 0.0 copy-done.3
  109.3 0.5 copy-done
  109.8 12.5 %fusion.7 = f32[8,128,896]{2,1,0:T(8,128)} fusion(bf16[1,4096,896]{2,1,0:T(8,128)(2,1)} %param.11, bf16[8,128,4096]{2,1,0:T(8,128)(2,1)S(1)} %copy-done, f32[4096]{0:T(1024)S(1)} %copy-done.3, f32[8,128]{1,0:T(8,128)S(1)} %add_rsqrt_fusion), kind=kOutput, calls=%fused_computation.10 | convolution fusion | flops 7532969984 | bytes 19419136 | tf_op jit(solution)/shard_map/slcd,ldf->slcf/dot_general | solution.py:39
  122.3 28.0 %fusion.3 = f32[8,128,4096]{2,1,0:T(8,128)} fusion(bf16[1,896,4096]{2,1,0:T(8,128)(2,1)} %param.13, f32[8,128,896]{2,1,0:T(8,128)} %fusion.7, bf16[1,4096,896]{2,1,0:T(8,128)(2,1)} %param.12, bf16[8,128,4096]{2,1,0:T(8,128)(2,1)} %all-gather.2.cloned.1.call-done, f32[4096]{0:T(1024)S(1)} %copy-done.3, f32[8,128]{1,0:T(8,128)S(1)} %add_rsqrt_fusion), kind=kOutput, calls=%fused_computation.6 | convolution fusion | flops 15054667776 | bytes 43536384 | tf_op jit(solution)/shard_map/slcf,lfd->slcd/dot_general | solution.py:44
  150.4 0.0 copy-start.2
  150.4 0.0 reduce-scatter.2.cloned.1.call-update
  150.4 0.0 copy-start.1
  150.4 144.8 %reduce-scatter.2.cloned.1.call-done = f32[8,128,256]{2,1,0:T(8,128)} async-done(((f32[8,128,4096]{2,1,0:T(8,128)}), f32[8,128,256]{2,1,0:T(8,128)}) %reduce-scatter.2.cloned.1.call-update) | async-done | bytes 1048592 | tf_op jit(solution)/shard_map/reduce_scatter | solution.py:58
  295.2 4.4 %all-to-all-start.1 = ((f32[8,128,256]{2,1,0:T(8,128)}), f32[8,128,256]{2,1,0:T(8,128)S(1)}, u32[]{:S(2)}, u32[]{:S(2)}) async-start(f32[8,128,256]{2,1,0:T(8,128)} %reduce-scatter.2.cloned.1.call-done), calls=%async_computation.2 | async-start | bytes 2097152 | tf_op jit(solution)/shard_map/all_to_all | solution.py:59
  299.6 0.1 copy.24
  299.7 0.1 reshape.72
  299.9 0.0 copy-done.2
  299.9 0.1 copy.25
  300.1 13.7 %all-to-all-done.1 = f32[8,128,256]{2,1,0:T(8,128)S(1)} async-done(((f32[8,128,256]{2,1,0:T(8,128)}), f32[8,128,256]{2,1,0:T(8,128)S(1)}, u32[]{:S(2)}, u32[]{:S(2)}) %all-to-all-start.1) | async-done | bytes 1048608 | tf_op jit(solution)/shard_map/all_to_all | solution.py:59
  313.8 1.6 gather_fusion
  315.4 0.3 reshape.71
  315.7 0.7 multiply_reduce_fusion
  316.4 0.0 copy-done.1
  316.4 0.7 add_convert_fusion
  (5 shorter events, 0.1 us)
Async XLA Ops:
  6.5 102.7 %copy-start.3 = (f32[4096]{0:T(1024)S(1)}, f32[4096]{0:T(1024)}, u32[]{:S(2)}) copy-start(f32[4096]{0:T(1024)} %param.8) | copy-start | bytes 49156
  6.5 97.5 %all-gather.2.cloned.1.call-start = ((), (), s32[]{:S(2)}) async-start(), calls=%async_computation.3 | async-start | bytes 8912896 | tf_op jit(solution)/shard_map/all_gather | solution.py:55
  27.9 267.2 %reduce-scatter.2.cloned.1.call-start = ((), (), s32[]{:S(2)}) async-start(), calls=%async_computation.4 | async-start | bytes 17825792 | tf_op jit(solution)/shard_map/reduce_scatter | solution.py:58
  104.0 5.8 %copy-start = (bf16[8,128,4096]{2,1,0:T(8,128)(2,1)S(1)}, bf16[8,128,4096]{2,1,0:T(8,128)(2,1)}, u32[]{:S(2)}) copy-start(bf16[8,128,4096]{2,1,0:T(8,128)(2,1)} %all-gather.2.cloned.1.call-done) | copy-start | bytes 25165828
  150.4 149.5 %copy-start.2 = (f32[256,2]{0,1:T(2,128)S(1)}, f32[256,2]{0,1:T(2,128)}, u32[]{:S(2)}) copy-start(f32[256,2]{0,1:T(2,128)} %param.10) | copy-start | bytes 6148
  150.4 166.0 %copy-start.1 = (bf16[256,256]{1,0:T(8,128)(2,1)S(1)}, bf16[256,256]{1,0:T(8,128)(2,1)}, u32[]{:S(2)}) copy-start(bf16[256,256]{1,0:T(8,128)(2,1)} %param.7) | copy-start | bytes 393220
  295.2 18.6 %all-to-all-start.1 = ((f32[8,128,256]{2,1,0:T(8,128)}), f32[8,128,256]{2,1,0:T(8,128)S(1)}, u32[]{:S(2)}, u32[]{:S(2)}) async-start(f32[8,128,256]{2,1,0:T(8,128)} %reduce-scatter.2.cloned.1.call-done), calls=%async_computation.2 | async-start | bytes 2097152 | tf_op jit(solution)/shard_map/all_to_all | solution.py:59
Sparse Core Ops, SparseCore 0:
  28.1 75.9 all-gather.1
  150.5 144.6 reduce-scatter.1
where the time goes:
time: 324 us
  waiting for transfers between devices  235 us (73%)
  matrix products  41.8 us (13%)
  blocking collectives  16.3 us (5%)
  between operations  13.5 us (4%)
  other arithmetic  8.85 us (3%)
  starting transfers between devices  4.49 us (1%)
  local copies, waits for them, and re-layouts  4.36 us (1%)
    reduce_scatter x1, waiting for transfers between devices, body(): shares = lax.psum_scatter(outputs, 'col', scatter_dimension=2, tiled=True)  145 us
    all_gather x1, waiting for transfers between devices, body(): widened = lax.all_gather(arrived, 'col', axis=2, tiled=True)  76 us
    dot_general x1, matrix products, run_experts(): jnp.einsum('slcf,lfd->slcd', hidden, down_block, preferred_element_type=j...  28 us
    all_to_all x1, blocking collectives, body(): lax.all_to_all(packed, 'row', split_axis=0, concat_axis=0, tiled=True)  16.3 us
    all_to_all x1, waiting for transfers between devices, body(): lax.all_to_all(shares, 'row', split_axis=0, concat_axis=0, tiled=True)  13.7 us
    dot_general x1, matrix products, run_experts(): jnp.einsum('slcd,ldf->slcf', grouped, gate_block, preferred_element_type=...  12.5 us
  transfers between devices with their start and end apart: 3, of which 3 were waited for; matrix products, arithmetic and copies ran while one was open for 0% of the time, Pallas kernels for 0%

commit v1 on v0

--- a/solution.py
+++ b/solution.py
@@ -52,7 +52,12 @@
     )
     packed = packed.reshape(EXPERTS, CAP, tokens.shape[1])
     arrived = lax.all_to_all(packed, "row", split_axis=0, concat_axis=0, tiled=True)
-    widened = lax.all_gather(arrived, "col", axis=2, tiled=True)
+
+    def space_begin(original, axis_tag, along_dim):
+        tall = lax.all_to_all(jnp.stack([original] * lax.axis_size(axis_tag)), axis_tag, 0, 0)
+        return jnp.concatenate(tall, along_dim)
+
+    widened = space_begin(arrived, "col", 2)
     normed = normalize(widened, norm_gain)
     outputs = run_experts(normed, w_gate, w_up, w_down)
     shares = lax.psum_scatter(outputs, "col", scatter_dimension=2, tiled=True)

time: 324 us -> 405 us (1.25)
  waiting for transfers between devices: 235 us -> 288 us
  local copies, waits for them, and re-layouts: 4.36 us -> 23.3 us
  starting transfers between devices: 4.49 us -> 11.6 us
    all_to_all x0 -> x1, waiting for transfers between devices: none -> 120 us  [space_begin(): lax.all_to_all(jnp.stack([original] * lax.axis_size(axis_tag)), axis_tag,...]
    all_gather x1 -> x0, waiting for transfers between devices: 76 us -> none  [body(): widened = lax.all_gather(arrived, 'col', axis=2, tiled=True)]
    all_to_all x0 -> x1, local copies, waits for them, and re-layouts: none -> 11.4 us  [space_begin(): lax.all_to_all(jnp.stack([original] * lax.axis_size(axis_tag)), axis_tag,...]
    reduce_scatter x1, waiting for transfers between devices: 145 us -> 154 us  [body(): shares = lax.psum_scatter(outputs, 'col', scatter_dimension=2, tiled=True)]
    all_to_all x0 -> x1, starting transfers between devices: none -> 6.92 us  [space_begin(): lax.all_to_all(jnp.stack([original] * lax.axis_size(axis_tag)), axis_tag,...]
    another operation x1 -> x2, local copies, waits for them, and re-layouts: 0.01 us -> 4.26 us  [the longest x1 4.26 us: space_begin(): jnp.stack([original] * lax.axis_size(axis_tag))]
where the time goes in v1:
time: 405 us
  waiting for transfers between devices  288 us (71%)
  matrix products  40.4 us (10%)
  local copies, waits for them, and re-layouts  23.3 us (6%)
  blocking collectives  16.2 us (4%)
  between operations  13.6 us (3%)
  other arithmetic  11.8 us (3%)
  starting transfers between devices  11.6 us (3%)
    reduce_scatter x1, waiting for transfers between devices, body(): shares = lax.psum_scatter(outputs, 'col', scatter_dimension=2, tiled=True)  154 us
    all_to_all x1, waiting for transfers between devices, space_begin(): lax.all_to_all(jnp.stack([original] * lax.axis_size(axis_tag)), axis_tag,...  120 us
    dot_general x1, matrix products, run_experts(): jnp.einsum('slcf,lfd->slcd', hidden, down_block, preferred_element_type=j...  28.1 us
    all_to_all x1, blocking collectives, body(): lax.all_to_all(packed, 'row', split_axis=0, concat_axis=0, tiled=True)  16.2 us
    all_to_all x1, waiting for transfers between devices, body(): lax.all_to_all(shares, 'row', split_axis=0, concat_axis=0, tiled=True)  13.8 us
    all_to_all x1, local copies, waits for them, and re-layouts, space_begin(): lax.all_to_all(jnp.stack([original] * lax.axis_size(axis_tag)), axis_tag,...  11.4 us
    dot_general x1, matrix products, run_experts(): jnp.einsum('slcd,ldf->slcf', grouped, gate_block, preferred_element_type=...  11 us
  transfers between devices with their start and end apart: 3, of which 3 were waited for; matrix products, arithmetic and copies ran while one was open for 0% of the time, Pallas kernels for 0%

profile of v1, /device:TPU:0, one launch (start us, length us, event | category | flops | bytes accessed | tf_op | source)
XLA Modules:
  0.0 404.6 jit_solution(4523859034384932434)
XLA Ops:
  6.5 0.8 copy.37
  7.3 0.1 eq.42
  7.5 0.1 eq.38
  7.7 1.1 reduce-window.6
  8.8 0.2 slice_reduce_fusion
  9.1 0.1 fusion.23
  9.1 0.1 reduce_sum.39
  9.3 0.1 copy.39
  9.4 0.7 compare_select_fusion
  10.1 0.3 convert_reduce_fusion
  10.3 1.3 convolution_convert_fusion
  11.6 16.2 %all_to_all.15 = bf16[8,128,256]{2,1,0:T(8,128)(2,1)S(1)} all-to-all(bf16[8,128,256]{2,1,0:T(8,128)(2,1)S(1)} %bitcast.74), channel_id=1, replica_groups=mesh['row'=8,'col'=16] {'row'}, dimensions={0} | all-to-all | bytes 1048576 | tf_op jit(solution)/shard_map/all_to_all | solution.py:54
  27.8 4.3 %stack.2 = bf16[16,8,128,256]{3,2,1,0:T(8,128)(2,1)} broadcast(bf16[8,128,256]{2,1,0:T(8,128)(2,1)S(1)} %all_to_all.15), dimensions={1,2,3} | broadcast | bytes 8912896 | tf_op jit(solution)/shard_map/stack | solution.py:57
  32.1 0.0 copy-start.3
  32.1 6.9 %all-to-all-start.1 = ((bf16[16,8,128,256]{3,2,1,0:T(8,128)(2,1)}), bf16[16,8,128,256]{3,2,1,0:T(8,128)(2,1)}, u32[]{:S(2)}, u32[]{:S(2)}) async-start(bf16[16,8,128,256]{3,2,1,0:T(8,128)(2,1)} %stack.2), calls=%async_computation.1 | async-start | bytes 16777216 | tf_op jit(solution)/shard_map/all_to_all | solution.py:57
  39.0 0.2 reduce-scatter.2.cloned.1.call-start
  39.2 0.0 copy-done.3
  39.2 119.8 %all-to-all-done.1 = bf16[16,8,128,256]{3,2,1,0:T(8,128)(2,1)} async-done(((bf16[16,8,128,256]{3,2,1,0:T(8,128)(2,1)}), bf16[16,8,128,256]{3,2,1,0:T(8,128)(2,1)}, u32[]{:S(2)}, u32[]{:S(2)}) %all-to-all-start.1) | async-done | bytes 8388640 | tf_op jit(solution)/shard_map/all_to_all | solution.py:57
  159.1 11.4 %copy.40 = bf16[16,8,128,256]{2,3,0,1:T(8,128)(2,1)} copy(bf16[16,8,128,256]{3,2,1,0:T(8,128)(2,1)} %all-to-all-done.1) | data formatting | bytes 16777216 | tf_op jit(solution)/shard_map/all_to_all | solution.py:57
  170.5 0.0 copy-start
  170.5 0.0 slice-start
  170.5 5.2 %fusion = f32[8,128]{1,0:T(8,128)S(1)} fusion(bf16[16,8,128,256]{2,3,0,1:T(8,128)(2,1)} %copy.40), kind=kLoop, calls=%fused_computation.3 | loop fusion | flops 12581888 | bytes 8392704 | tf_op jit(solution)/shard_map/reduce_sum | solution.py:12
  175.7 0.6 copy-done
  176.3 0.0 slice-start.1
  176.3 3.0 fusion.2
  179.3 0.0 copy-start.1
  179.3 3.2 copy-done.1
  182.5 0.0 slice-done
  182.5 0.0 slice-done.1
  182.5 11.0 %fusion.7 = f32[8,128,896]{2,1,0:T(8,128)} fusion(bf16[8,128,4096]{1,2,0:T(8,128)(2,1)S(1)} %bitcast.71, bf16[1,4096,896]{2,1,0:T(8,128)(2,1)S(1)} %bitcast.76), kind=kOutput, calls=%fused_computation.10 | convolution fusion | flops 7516192768 | bytes 19398656 | tf_op jit(solution)/shard_map/slcd,ldf->slcf/dot_general | solution.py:39
  193.5 28.1 %fusion.3 = f32[8,128,4096]{2,1,0:T(8,128)} fusion(bf16[1,896,4096]{2,1,0:T(8,128)(2,1)} %param.13, f32[8,128,896]{2,1,0:T(8,128)} %fusion.7, bf16[8,128,4096]{1,2,0:T(8,128)(2,1)} %bitcast.72, bf16[1,4096,896]{2,1,0:T(8,128)(2,1)} %param.12), kind=kOutput, calls=%fused_computation.6 | convolution fusion | flops 15037890560 | bytes 43515904 | tf_op jit(solution)/shard_map/slcf,lfd->slcd/dot_general | solution.py:44
  221.6 0.0 copy-start.4
  221.6 0.0 reduce-scatter.2.cloned.1.call-update
  221.7 0.0 copy-start.2
  221.7 154.1 %reduce-scatter.2.cloned.1.call-done = f32[8,128,256]{2,1,0:T(8,128)} async-done(((f32[8,128,4096]{2,1,0:T(8,128)}), f32[8,128,256]{2,1,0:T(8,128)}) %reduce-scatter.2.cloned.1.call-update) | async-done | bytes 1048592 | tf_op jit(solution)/shard_map/reduce_scatter | solution.py:63
  375.8 4.4 %all-to-all-start.2 = ((f32[8,128,256]{2,1,0:T(8,128)}), f32[8,128,256]{2,1,0:T(8,128)S(1)}, u32[]{:S(2)}, u32[]{:S(2)}) async-start(f32[8,128,256]{2,1,0:T(8,128)} %reduce-scatter.2.cloned.1.call-done), calls=%async_computation.3 | async-start | bytes 2097152 | tf_op jit(solution)/shard_map/all_to_all | solution.py:64
  380.2 0.1 copy.43
  380.3 0.1 reshape.82
  380.5 0.0 copy-done.4
  380.5 0.1 copy.44
  380.7 13.8 %all-to-all-done.2 = f32[8,128,256]{2,1,0:T(8,128)S(1)} async-done(((f32[8,128,256]{2,1,0:T(8,128)}), f32[8,128,256]{2,1,0:T(8,128)S(1)}, u32[]{:S(2)}, u32[]{:S(2)}) %all-to-all-start.2) | async-done | bytes 1048608 | tf_op jit(solution)/shard_map/all_to_all | solution.py:64
  394.4 1.6 gather_fusion
  396.0 0.3 reshape.81
  396.3 0.7 multiply_reduce_fusion
  397.0 0.0 copy-done.2
  397.0 0.7 add_convert_fusion
  (7 shorter events, 0.1 us)
Async XLA Ops:
  32.1 7.2 %copy-start.3 = (f32[4096]{0:T(1024)S(1)}, f32[4096]{0:T(1024)}, u32[]{:S(2)}) copy-start(f32[4096]{0:T(1024)} %param.8) | copy-start | bytes 49156
  32.1 127.0 %all-to-all-start.1 = ((bf16[16,8,128,256]{3,2,1,0:T(8,128)(2,1)}), bf16[16,8,128,256]{3,2,1,0:T(8,128)(2,1)}, u32[]{:S(2)}, u32[]{:S(2)}) async-start(bf16[16,8,128,256]{3,2,1,0:T(8,128)(2,1)} %stack.2), calls=%async_computation.1 | async-start | bytes 16777216 | tf_op jit(solution)/shard_map/all_to_all | solution.py:57
  39.0 336.8 %reduce-scatter.2.cloned.1.call-start = ((), (), s32[]{:S(2)}) async-start(), calls=%async_computation.4 | async-start | bytes 17825792 | tf_op jit(solution)/shard_map/reduce_scatter | solution.py:63
  170.5 5.8 %copy-start = (bf16[16,8,128,256]{2,3,0,1:T(8,128)(2,1)S(1)}, bf16[16,8,128,256]{2,3,0,1:T(8,128)(2,1)}, u32[]{:S(2)}) copy-start(bf16[16,8,128,256]{2,3,0,1:T(8,128)(2,1)} %copy.40) | copy-start | bytes 25165828
  170.5 12.0 %slice-start = ((s8[7340032]{0:T(1024)(128)(4,1)}), s8[3145728]{0:T(1024)(128)(4,1)S(1)}, s32[]{:S(2)}) async-start(s8[7340032]{0:T(1024)(128)(4,1)} %bitcast.75), calls=%async_computation.5 | async-start | bytes 6291456
  176.3 6.2 %slice-start.1 = ((s8[7340032]{0:T(1024)(128)(4,1)}), s8[4194304]{0:T(1024)(128)(4,1)S(1)}, s32[]{:S(2)}) async-start(s8[7340032]{0:T(1024)(128)(4,1)} %bitcast.75), calls=%async_computation.6 | async-start | bytes 8388608
  179.3 3.2 copy-start.1
  221.6 158.9 %copy-start.4 = (f32[256,2]{0,1:T(2,128)S(1)}, f32[256,2]{0,1:T(2,128)}, u32[]{:S(2)}) copy-start(f32[256,2]{0,1:T(2,128)} %param.10) | copy-start | bytes 6148
  221.7 175.4 %copy-start.2 = (bf16[256,256]{1,0:T(8,128)(2,1)S(1)}, bf16[256,256]{1,0:T(8,128)(2,1)}, u32[]{:S(2)}) copy-start(bf16[256,256]{1,0:T(8,128)(2,1)} %param.7) | copy-start | bytes 393220
  375.8 18.7 %all-to-all-start.2 = ((f32[8,128,256]{2,1,0:T(8,128)}), f32[8,128,256]{2,1,0:T(8,128)S(1)}, u32[]{:S(2)}, u32[]{:S(2)}) async-start(f32[8,128,256]{2,1,0:T(8,128)} %reduce-scatter.2.cloned.1.call-done), calls=%async_computation.3 | async-start | bytes 2097152 | tf_op jit(solution)/shard_map/all_to_all | solution.py:64
Sparse Core Ops, SparseCore 0:
  221.8 153.9 reduce-scatter.1
